TPU v7x, 32 devices: a whole 2x2x4 slice. The times are simulated.
32 devices in a mesh: vp: 8 (over z, x), ch: 4 (over y, core).
Axes of the slice: x: 2, y: 2, z: 4, core: 2. Of those that a mesh axis runs over, the one named last changes fastest.
Arguments:
- chol_a: bfloat16 [640, 4, 6000], P('vp', None, 'ch'), may hold values from -0.078125 to 0.078125
- chol_b: bfloat16 [6000, 8, 640], P('ch', 'vp'), may hold values from -6 to 6
- amplitudes: bfloat16 [640, 8, 640], P('vp'), may hold values from -0.0390625 to 0.0390625
- vir_a: float32 [4], replicated, may hold values from 0.2 to 3
- vir_b: float32 [8], P('vp'), may hold values from 0.2 to 3
- occ_pair: float32 [8], P('ch'), may hold values from -4 to -1
Outputs:
- increment: float32 [4, 8, 8], P(None, 'vp', 'ch')
All inputs are finite; a program needn't handle non-finite values.
Results may differ from a plain program's by a relative error of at most 0.0029.
Values may be sent and summed in bfloat16 or wider, within the bound.
No kernel may reach another device: no remote copies, remote signals or barrier semaphores. Data moves between devices by JAX's collectives and lax.ppermute only.
A program may use at most 64 MiB of HBM per device.

v0:
```python
import jax
import jax.numpy as jnp
from jax import lax
from jax.sharding import PartitionSpec as P


def body(chol_a, chol_b, amplitudes, vir_a, vir_b, occ_pair):
    nch_dev = chol_b.shape[0]
    nb_dev = chol_b.shape[1]
    vir_count = chol_b.shape[2]
    a_count = chol_a.shape[1]
    pair_count = amplitudes.shape[1]
    cholesky_right = chol_b.reshape(nch_dev, nb_dev * vir_count)
    panel_rows = lax.all_gather(chol_a, "vp", axis=0, tiled=True)
    rows_here = panel_rows.shape[0]
    v_rows = jnp.dot(
        panel_rows.reshape(rows_here * a_count, nch_dev),
        cholesky_right,
        preferred_element_type=jnp.float32,
    )
    v_all = v_rows.astype(jnp.bfloat16).reshape(rows_here, a_count * nb_dev, vir_count)
    quarter = pair_count // lax.axis_size("ch")
    own_pairs = lax.dynamic_slice_in_dim(amplitudes, lax.axis_index("ch") * quarter, quarter, 1)
    spread = lax.all_gather(own_pairs, "vp", axis=0, tiled=True)
    all_pairs = lax.all_gather(spread, "ch", axis=1, tiled=True)
    ladder = jnp.einsum("cxd,cid->xi", v_all, all_pairs, preferred_element_type=jnp.float32)
    ladder = ladder.reshape(a_count, nb_dev, pair_count)
    ladder = lax.psum_scatter(ladder, "ch", scatter_dimension=2, tiled=True)
    energy_gap = vir_a[:, None, None] + vir_b[None, :, None] - occ_pair[None, None, :]
    return ladder / energy_gap


def solution(mesh):
    return jax.shard_map(
        body,
        mesh=mesh,
        in_specs=(
            P("vp", None, "ch"),
            P("ch", "vp", None),
            P("vp", None, None),
            P(),
            P("vp"),
            P("ch"),
        ),
        out_specs=P(None, "vp", "ch"),
        check_vma=False,
    )
```

profile of v0, /device:TPU:0, one launch (start us, length us, event | category | flops | bytes accessed | tf_op | source)
XLA Modules:
  0.0 245.8 jit_solution(5086026645808385693)
XLA Ops:
  6.5 0.0 copy-start
  6.5 0.0 all-gather.6.cloned.1.call-start
  6.5 0.0 copy-start.3
  6.5 0.0 copy-start.2
  6.5 2.2 constant_dynamic-slice_fusion.1
  8.7 0.0 all-gather.6.cloned.1.call-update
  8.8 0.0 all-gather.4.cloned.1.call-start
  8.8 0.7 all-gather.4.cloned.1.call-update
  9.5 0.0 all-gather.8.cloned.1.call-start
  9.6 47.5 %all-gather.6.cloned.1.call-done = bf16[640,2,640]{2,1,0:T(2,128)(2,1)} async-done(((bf16[80,2,640]{2,1,0:T(2,128)(2,1)}), bf16[640,2,640]{2,1,0:T(2,128)(2,1)}) %all-gather.6.cloned.1.call-update) | async-done | bytes 1638416 | tf_op jit(solution)/shard_map/all_gather | solution.py:24
  57.1 2.8 %copy.13 = bf16[640,2,640]{2,0,1:T(8,128)(2,1)} copy(bf16[640,2,640]{2,1,0:T(2,128)(2,1)} %all-gather.6.cloned.1.call-done) | data formatting | bytes 3276800 | tf_op jit(solution)/shard_map/all_gather | solution.py:24
  59.9 0.0 all-gather.8.cloned.1.call-update
  60.6 0.0 copy-done.3
  60.6 0.6 dynamic-slice
  61.8 0.0 copy-done.2
  61.9 113.8 %all-gather.4.cloned.1.call-done = bf16[640,4,1500]{2,1,0:T(4,128)(2,1)} async-done(((bf16[80,4,1500]{2,1,0:T(4,128)(2,1)}), bf16[640,4,1500]{2,1,0:T(4,128)(2,1)}) %all-gather.4.cloned.1.call-update) | async-done | bytes 7680016 | tf_op jit(solution)/shard_map/all_gather | solution.py:14
  175.6 13.5 %reshape.60 = bf16[2560,1500]{1,0:T(8,128)(2,1)} reshape(bf16[640,4,1500]{2,1,0:T(4,128)(2,1)} %all-gather.4.cloned.1.call-done) | data formatting | bytes 15360000 | tf_op jit(solution)/shard_map/reshape | solution.py:17
  189.1 0.0 copy-done
  189.1 9.8 %convolution_convert_fusion = bf16[2560,640]{1,0:T(8,128)(2,1)} fusion(bf16[2560,1500]{1,0:T(8,128)(2,1)} %reshape.60, bf16[1500,1,640]{2,0,1:T(8,128)(2,1)S(1)} %copy-done), kind=kOutput, calls=%fused_computation.2 | convolution fusion | flops 4916838400 | bytes 12876800 | tf_op jit(solution)/shard_map/dot_general | solution.py:16
  198.9 6.5 %reshape.62 = bf16[640,4,640]{2,1,0:T(4,128)(2,1)} reshape(bf16[2560,640]{1,0:T(8,128)(2,1)} %convolution_convert_fusion) | data formatting | bytes 6553600 | tf_op jit(solution)/shard_map/reshape | solution.py:21
  205.4 0.0 copy-start.1
  205.4 17.9 %all-gather.8.cloned.1.call-done = bf16[640,8,640]{2,0,1:T(8,128)(2,1)} async-done(((bf16[640,2,640]{2,0,1:T(8,128)(2,1)}), bf16[640,8,640]{2,0,1:T(8,128)(2,1)}) %all-gather.8.cloned.1.call-update) | async-done | bytes 6553616 | tf_op jit(solution)/shard_map/all_gather | solution.py:25
  223.3 9.5 %fusion = f32[4,8,1]{0,1,2:T(8,128)S(1)} fusion(bf16[640,4,640]{2,1,0:T(4,128)(2,1)} %reshape.62, bf16[640,8,640]{2,0,1:T(8,128)(2,1)} %all-gather.8.cloned.1.call-done), kind=kOutput, calls=%fused_computation | convolution fusion | flops 26214400 | bytes 9830528 | tf_op jit(solution)/shard_map/cxd,cid->xi/dot_general | solution.py:26
  232.7 5.9 %all-reduce = f32[4,1,8]{0,1,2:T(1,128)S(1)} all-reduce(f32[4,1,8]{0,1,2:T(1,128)S(1)} %bitcast.13), channel_id=2, replica_groups=mesh['vp'=8,'ch'=4] {'ch'}, use_global_device_ids=true, to_apply=%region_0.0.clone | all-reduce | flops 32 | bytes 256
  238.6 0.0 copy-done.1
  238.6 0.6 subtract_divide_fusion
  (2 shorter events, 0.0 us)
Async XLA Ops:
  6.5 182.5 %copy-start = (bf16[1500,1,640]{2,0,1:T(8,128)(2,1)S(1)}, bf16[1500,1,640]{2,0,1:T(8,128)(2,1)}, u32[]{:S(2)}) copy-start(bf16[1500,1,640]{2,0,1:T(8,128)(2,1)} %param.7) | copy-start | bytes 5760004
  6.5 50.6 %all-gather.6.cloned.1.call-start = ((), (), s32[]{:S(2)}) async-start(), calls=%async_computation.1 | async-start | bytes 1843200 | tf_op jit(solution)/shard_map/all_gather | solution.py:24
  6.5 54.1 %copy-start.3 = (u32[32]{0:T(128)S(1)}, u32[32]{0:T(128)}, u32[]{:S(2)}) copy-start(u32[32]{0:T(128)} %constant.15) | copy-start | bytes 388
  6.5 55.3 %copy-start.2 = (f32[4]{0:T(128)S(1)}, f32[4]{0:T(128)}, u32[]{:S(2)}) copy-start(f32[4]{0:T(128)} %param.9) | copy-start | bytes 52
  8.8 166.9 %all-gather.4.cloned.1.call-start = ((), (), s32[]{:S(2)}) async-start(), calls=%async_computation | async-start | bytes 8847360 | tf_op jit(solution)/shard_map/all_gather | solution.py:14
  9.5 213.7 %all-gather.8.cloned.1.call-start = ((), (), s32[]{:S(2)}) async-start(), calls=%async_computation.2 | async-start | bytes 8192000 | tf_op jit(solution)/shard_map/all_gather | solution.py:25
  205.4 33.3 %copy-start.1 = (f32[2]{0:T(128)S(1)}, f32[2]{0:T(128)}, u32[]{:S(2)}) copy-start(f32[2]{0:T(128)} %param.11) | copy-start | bytes 28
Sparse Core Ops, SparseCore 0:
  9.5 47.5 all-gather.5
  59.3 116.2 all-gather.3
  177.2 46.0 all-gather.7
where the time goes:
time: 246 us
  waiting for transfers between devices  180 us (73%)
  local copies, waits for them, and re-layouts  25.6 us (10%)
  matrix products  19.3 us (8%)
  between operations  14.4 us (6%)
  blocking collectives  5.89 us (2%)
    all_gather x1, waiting for transfers between devices, body(): panel_rows = lax.all_gather(chol_a, 'vp', axis=0, tiled=True)  114 us
    all_gather x1, waiting for transfers between devices, body(): spread = lax.all_gather(own_pairs, 'vp', axis=0, tiled=True)  47.5 us
    all_gather x1, waiting for transfers between devices, body(): all_pairs = lax.all_gather(spread, 'ch', axis=1, tiled=True)  17.9 us
    reshape x1, local copies, waits for them, and re-layouts, body(): panel_rows.reshape(rows_here * a_count, nch_dev)  13.5 us
    dot_general x1, matrix products, body(): jnp.dot(panel_rows.reshape(rows_here * a_count, nch_dev), cholesky_right,...  9.8 us
    dot_general x1, matrix products, body(): jnp.einsum('cxd,cid->xi', v_all, all_pairs, preferred_element_type=jnp.fl...  9.47 us
    reshape x1, local copies, waits for them, and re-layouts, body(): v_rows.astype(jnp.bfloat16).reshape(rows_here, a_count * nb_dev, vir_count)  6.49 us
    unnamed x1, blocking collectives  5.89 us
  transfers between devices with their start and end apart: 3, of which 3 were waited for; matrix products, arithmetic and copies ran while one was open for 13% of the time, Pallas kernels for 0%

commit v1 on v0

--- a/solution.py
+++ b/solution.py
@@ -11,7 +11,12 @@
     a_count = chol_a.shape[1]
     pair_count = amplitudes.shape[1]
     cholesky_right = chol_b.reshape(nch_dev, nb_dev * vir_count)
-    panel_rows = lax.all_gather(chol_a, "vp", axis=0, tiled=True)
+    ring = [chol_a]
+    for hop in range(7):
+        ring.append(lax.ppermute(ring[-1], "vp", [(dev, (dev + 1) % 8) for dev in range(8)]))
+    panel_rows = jnp.roll(
+        jnp.concatenate(ring[::-1], axis=0), (lax.axis_index("vp") + 1) * ring[0].shape[0], axis=0
+    )
     rows_here = panel_rows.shape[0]
     v_rows = jnp.dot(
         panel_rows.reshape(rows_here * a_count, nch_dev),

time: 246 us -> 296 us (1.20)
  local copies, waits for them, and re-layouts: 25.6 us -> 72.1 us
    ppermute x0 -> x7, waiting for transfers between devices: none -> 179 us  [body(): lax.ppermute(ring[-1], 'vp', [(dev, (dev + 1) % 8) for dev in range(8)])]
    all_gather x1 -> x0, waiting for transfers between devices: 114 us -> none  [body(): panel_rows = lax.all_gather(chol_a, 'vp', axis=0, tiled=True)]
    all_gather x1, waiting for transfers between devices: 47.5 us -> 0.01 us  [body(): spread = lax.all_gather(own_pairs, 'vp', axis=0, tiled=True)]
    unnamed x10 -> x31, local copies, waits for them, and re-layouts: 0.61 us -> 37.2 us
    all_gather x1, waiting for transfers between devices: 17.9 us -> 0.01 us  [body(): all_pairs = lax.all_gather(spread, 'ch', axis=1, tiled=True)]
    dynamic_slice x0 -> x1, local copies, waits for them, and re-layouts: none -> 9.08 us  [body(): jnp.roll(jnp.concatenate(ring[::-1], axis=0), (lax.axis_index('vp') + 1)...]
    ppermute x0 -> x7, starting transfers between devices: none -> 2.98 us  [body(): lax.ppermute(ring[-1], 'vp', [(dev, (dev + 1) % 8) for dev in range(8)])]
  transfers between devices with their start and end apart: 3 -> 9, of which waited for: 3 -> 7; matrix products, arithmetic and copies ran while one was open for 13% -> 27% of each run, Pallas kernels for 0% -> 0%
where the time goes in v1:
time: 296 us; the launch traced here: 295 us
  waiting for transfers between devices  179 us (60%)
  local copies, waits for them, and re-layouts  72.1 us (24%)
  matrix products  19.2 us (6%)
  between operations  14.8 us (5%)
  blocking collectives  5.89 us (2%)
  starting transfers between devices  3.03 us (1%)
    ppermute x7, waiting for transfers between devices, body(): lax.ppermute(ring[-1], 'vp', [(dev, (dev + 1) % 8) for dev in range(8)])  179 us
    unnamed x31, local copies, waits for them, and re-layouts  37.2 us
    reshape x1, local copies, waits for them, and re-layouts, body(): panel_rows.reshape(rows_here * a_count, nch_dev)  13.2 us
    dot_general x1, matrix products, body(): jnp.dot(panel_rows.reshape(rows_here * a_count, nch_dev), cholesky_right,...  9.74 us
    dot_general x1, matrix products, body(): jnp.einsum('cxd,cid->xi', v_all, all_pairs, preferred_element_type=jnp.fl...  9.47 us
    dynamic_slice x1, local copies, waits for them, and re-layouts, body(): jnp.roll(jnp.concatenate(ring[::-1], axis=0), (lax.axis_index('vp') + 1)...  9.08 us
    reshape x1, local copies, waits for them, and re-layouts, body(): v_rows.astype(jnp.bfloat16).reshape(rows_here, a_count * nb_dev, vir_count)  6.51 us
  transfers between devices with their start and end apart: 9, of which 7 were waited for; matrix products, arithmetic and copies ran while one was open for 27% of the time, Pallas kernels for 0%

profile of v1, /device:TPU:0, one launch (start us, length us, event | category | flops | bytes accessed | tf_op | source)
XLA Modules:
  0.0 295.2 jit_solution(8753736666226934506)
XLA Ops:
  6.5 0.0 copy-start
  6.5 0.0 copy-start.1
  6.5 0.0 all-gather.3.cloned.1.call-start
  6.5 3.0 %collective-permute-start = (bf16[80,4,1500]{2,1,0:T(4,128)(2,1)}, bf16[80,4,1500]{2,1,0:T(4,128)(2,1)}, u32[]{:S(2)}, u32[]{:S(2)}) collective-permute-start(bf16[80,4,1500]{2,1,0:T(4,128)(2,1)} %param.6), channel_id=1, source_target_pairs={{0,4},{4,8},{8,12},{12,16},{16,20},{20,24},{24,28},{28,0},{1,5},{5... | collective-permute-start | bytes 2880008 | tf_op jit(solution)/shard_map/ppermute | solution.py:16
  9.5 2.0 constant_dynamic-slice_fusion.1
  11.5 0.0 all-gather.3.cloned.1.call-update
  11.6 0.0 all-gather.5.cloned.1.call-start
  11.6 29.6 %collective-permute-done = bf16[80,4,1500]{2,1,0:T(4,128)(2,1)} collective-permute-done((bf16[80,4,1500]{2,1,0:T(4,128)(2,1)}, bf16[80,4,1500]{2,1,0:T(4,128)(2,1)}, u32[]{:S(2)}, u32[]{:S(2)}) %collective-permute-start) | collective-permute-done | bytes 960032 | tf_op jit(solution)/shard_map/ppermute | solution.py:16
  41.2 0.0 collective-permute-start.1
  41.2 39.1 %collective-permute-done.1 = bf16[80,4,1500]{2,1,0:T(4,128)(2,1)S(1)} collective-permute-done((bf16[80,4,1500]{2,1,0:T(4,128)(2,1)}, bf16[80,4,1500]{2,1,0:T(4,128)(2,1)S(1)}, u32[]{:S(2)}, u32[]{:S(2)}) %collective-permute-start.1) | collective-permute-done | bytes 960032 | tf_op jit(solution)/shard_map/ppermute | solution.py:16
  80.3 0.0 copy-start.2
  80.3 0.9 copy-done.2
  81.3 0.0 collective-permute-start.2
  81.3 24.9 %collective-permute-done.2 = bf16[80,4,1500]{2,1,0:T(4,128)(2,1)} collective-permute-done((bf16[80,4,1500]{2,1,0:T(4,128)(2,1)S(1)}, bf16[80,4,1500]{2,1,0:T(4,128)(2,1)}, u32[]{:S(2)}, u32[]{:S(2)}) %collective-permute-start.2) | collective-permute-done | bytes 960032 | tf_op jit(solution)/shard_map/ppermute | solution.py:16
  106.1 0.0 collective-permute-start.3
  106.1 0.0 all-gather.3.cloned.1.call-done
  106.1 2.8 copy.13
  108.9 0.0 all-gather.5.cloned.1.call-update
  109.0 21.4 %collective-permute-done.3 = bf16[80,4,1500]{2,1,0:T(4,128)(2,1)} collective-permute-done((bf16[80,4,1500]{2,1,0:T(4,128)(2,1)}, bf16[80,4,1500]{2,1,0:T(4,128)(2,1)}, u32[]{:S(2)}, u32[]{:S(2)}) %collective-permute-start.3) | collective-permute-done | bytes 960032 | tf_op jit(solution)/shard_map/ppermute | solution.py:16
  130.3 0.0 collective-permute-start.4
  130.3 23.3 %collective-permute-done.4 = bf16[80,4,1500]{2,1,0:T(4,128)(2,1)S(1)} collective-permute-done((bf16[80,4,1500]{2,1,0:T(4,128)(2,1)}, bf16[80,4,1500]{2,1,0:T(4,128)(2,1)S(1)}, u32[]{:S(2)}, u32[]{:S(2)}) %collective-permute-start.4) | collective-permute-done | bytes 960032 | tf_op jit(solution)/shard_map/ppermute | solution.py:16
  153.6 0.0 copy-start.4
  153.6 1.0 copy-done.4
  154.5 0.0 collective-permute-start.5
  154.6 22.3 %collective-permute-done.5 = bf16[80,4,1500]{2,1,0:T(4,128)(2,1)} collective-permute-done((bf16[80,4,1500]{2,1,0:T(4,128)(2,1)S(1)}, bf16[80,4,1500]{2,1,0:T(4,128)(2,1)}, u32[]{:S(2)}, u32[]{:S(2)}) %collective-permute-start.5) | collective-permute-done | bytes 960032 | tf_op jit(solution)/shard_map/ppermute | solution.py:16
  176.8 0.0 collective-permute-start.6
  177.5 1.2 dynamic-slice
  179.4 0.0 copy-start.5
  179.4 0.0 copy-start.3
  179.4 0.8 broadcast_add_fusion
  180.2 18.3 %collective-permute-done.6 = bf16[80,4,1500]{2,1,0:T(4,128)(2,1)} collective-permute-done((bf16[80,4,1500]{2,1,0:T(4,128)(2,1)}, bf16[80,4,1500]{2,1,0:T(4,128)(2,1)}, u32[]{:S(2)}, u32[]{:S(2)}) %collective-permute-start.6) | collective-permute-done | bytes 960032 | tf_op jit(solution)/shard_map/ppermute | solution.py:16
  198.5 2.5 constant_dynamic-update-slice_fusion.15
  201.0 2.5 constant_dynamic-update-slice_fusion.14
  203.5 2.5 constant_dynamic-update-slice_fusion.13
  206.0 2.5 constant_dynamic-update-slice_fusion.12
  208.5 2.5 constant_dynamic-update-slice_fusion.11
  211.0 2.5 constant_dynamic-update-slice_fusion.10
  213.5 2.5 constant_dynamic-update-slice_fusion.9
  216.0 0.0 copy-done.1
  216.0 1.3 constant_dynamic-update-slice_fusion.8
  217.3 2.6 constant_dynamic-update-slice_fusion.7
  219.9 2.5 constant_dynamic-update-slice_fusion.6
  222.3 0.0 copy-done.5
  222.3 1.3 constant_dynamic-update-slice_fusion.5
  223.6 2.5 constant_dynamic-update-slice_fusion.4
  226.1 2.5 constant_dynamic-update-slice_fusion.3
  228.7 0.0 copy-done.3
  228.7 1.4 constant_dynamic-update-slice_fusion.2
  230.0 2.5 constant_dynamic-update-slice_fusion.1
  232.5 1.3 constant_dynamic-update-slice_fusion
  233.8 9.1 %constant_dynamic-slice_fusion.2 = bf16[640,4,1500]{2,1,0:T(4,128)(2,1)} fusion(bf16[1280,4,1500]{2,1,0:T(4,128)(2,1)} %constant_dynamic-update-slice_fusion, s32[]{:T(128)S(6)} %select_n.17), kind=kLoop, calls=%fused_computation.23 | loop fusion | bytes 15360004 | tf_op jit(solution)/shard_map/jit(_roll_dynamic)/dynamic_slice | solution.py:17
  242.9 13.2 %reshape.60 = bf16[2560,1500]{1,0:T(8,128)(2,1)} reshape(bf16[640,4,1500]{2,1,0:T(4,128)(2,1)} %constant_dynamic-slice_fusion.2) | data formatting | bytes 15360000 | tf_op jit(solution)/shard_map/reshape | solution.py:22
  256.1 0.0 copy-done
  256.1 9.7 %convolution_convert_fusion = bf16[2560,640]{1,0:T(8,128)(2,1)} fusion(bf16[2560,1500]{1,0:T(8,128)(2,1)} %reshape.60, bf16[1500,1,640]{2,0,1:T(8,128)(2,1)S(1)} %copy-done), kind=kOutput, calls=%fused_computation.2 | convolution fusion | flops 4916838400 | bytes 12876800 | tf_op jit(solution)/shard_map/dot_general | solution.py:21
  265.9 0.0 copy-start.6
  265.9 6.5 %reshape.62 = bf16[640,4,640]{2,1,0:T(4,128)(2,1)} reshape(bf16[2560,640]{1,0:T(8,128)(2,1)} %convolution_convert_fusion) | data formatting | bytes 6553600 | tf_op jit(solution)/shard_map/reshape | solution.py:26
  272.4 0.0 all-gather.5.cloned.1.call-done
  272.4 9.5 %fusion = f32[4,8,1]{0,1,2:T(8,128)S(1)} fusion(bf16[640,4,640]{2,1,0:T(4,128)(2,1)} %reshape.62, bf16[640,8,640]{2,0,1:T(8,128)(2,1)} %all-gather.5.cloned.1.call-done), kind=kOutput, calls=%fused_computation | convolution fusion | flops 26214400 | bytes 9830528 | tf_op jit(solution)/shard_map/cxd,cid->xi/dot_general | solution.py:31
  281.8 5.9 %all-reduce = f32[4,1,8]{0,1,2:T(1,128)S(1)} all-reduce(f32[4,1,8]{0,1,2:T(1,128)S(1)} %bitcast.13), channel_id=2, replica_groups=mesh['vp'=8,'ch'=4] {'ch'}, use_global_device_ids=true, to_apply=%region_0.1.clone | all-reduce | flops 32 | bytes 256
  287.7 0.0 copy-done.6
  287.7 0.6 subtract_divide_fusion
  (1 shorter events, 0.0 us)
Async XLA Ops:
  6.5 249.6 %copy-start = (bf16[1500,1,640]{2,0,1:T(8,128)(2,1)S(1)}, bf16[1500,1,640]{2,0,1:T(8,128)(2,1)}, u32[]{:S(2)}) copy-start(bf16[1500,1,640]{2,0,1:T(8,128)(2,1)} %param.7) | copy-start | bytes 5760004
  6.5 209.5 %copy-start.1 = (bf16[80,4,1500]{2,1,0:T(4,128)(2,1)S(1)}, bf16[80,4,1500]{2,1,0:T(4,128)(2,1)}, u32[]{:S(2)}) copy-start(bf16[80,4,1500]{2,1,0:T(4,128)(2,1)} %param.6) | copy-start | bytes 2880004
  6.5 99.6 %all-gather.3.cloned.1.call-start = ((), (), s32[]{:S(2)}) async-start(), calls=%async_computation | async-start | bytes 1843200 | tf_op jit(solution)/shard_map/all_gather | solution.py:29
  6.5 34.7 %collective-permute-start = (bf16[80,4,1500]{2,1,0:T(4,128)(2,1)}, bf16[80,4,1500]{2,1,0:T(4,128)(2,1)}, u32[]{:S(2)}, u32[]{:S(2)}) collective-permute-start(bf16[80,4,1500]{2,1,0:T(4,128)(2,1)} %param.6), channel_id=1, source_target_pairs={{0,4},{4,8},{8,12},{12,16},{16,20},{20,24},{24,28},{28,0},{1,5},{5... | collective-permute-start | bytes 2880008 | tf_op jit(solution)/shard_map/ppermute | solution.py:16
  11.6 260.8 %all-gather.5.cloned.1.call-start = ((), (), s32[]{:S(2)}) async-start(), calls=%async_computation.1 | async-start | bytes 8192000 | tf_op jit(solution)/shard_map/all_gather | solution.py:30
  41.2 39.1 %collective-permute-start.1 = (bf16[80,4,1500]{2,1,0:T(4,128)(2,1)}, bf16[80,4,1500]{2,1,0:T(4,128)(2,1)S(1)}, u32[]{:S(2)}, u32[]{:S(2)}) collective-permute-start(bf16[80,4,1500]{2,1,0:T(4,128)(2,1)} %collective-permute-done), channel_id=1, source_target_pairs={{0,4},{4,8},{8,12},{12,16},{16,20},{20,24},{24,28},{28,0},{1,5},{5... | collective-permute-start | bytes 2880008 | tf_op jit(solution)/shard_map/ppermute | solution.py:16
  80.3 0.9 copy-start.2
  81.3 24.9 %collective-permute-start.2 = (bf16[80,4,1500]{2,1,0:T(4,128)(2,1)S(1)}, bf16[80,4,1500]{2,1,0:T(4,128)(2,1)}, u32[]{:S(2)}, u32[]{:S(2)}) collective-permute-start(bf16[80,4,1500]{2,1,0:T(4,128)(2,1)S(1)} %collective-permute-done.1), channel_id=1, source_target_pairs={{0,4},{4,8},{8,12},{12,16},{16,20},{20,24},{24,28},{28,0},{1,5},{5... | collective-permute-start | bytes 2880008 | tf_op jit(solution)/shard_map/ppermute | solution.py:16
  106.1 24.2 %collective-permute-start.3 = (bf16[80,4,1500]{2,1,0:T(4,128)(2,1)}, bf16[80,4,1500]{2,1,0:T(4,128)(2,1)}, u32[]{:S(2)}, u32[]{:S(2)}) collective-permute-start(bf16[80,4,1500]{2,1,0:T(4,128)(2,1)} %collective-permute-done.2), channel_id=1, source_target_pairs={{0,4},{4,8},{8,12},{12,16},{16,20},{20,24},{24,28},{28,0},{1,5},{5... | collective-permute-start | bytes 2880008 | tf_op jit(solution)/shard_map/ppermute | solution.py:16
  130.3 23.3 %collective-permute-start.4 = (bf16[80,4,1500]{2,1,0:T(4,128)(2,1)}, bf16[80,4,1500]{2,1,0:T(4,128)(2,1)S(1)}, u32[]{:S(2)}, u32[]{:S(2)}) collective-permute-start(bf16[80,4,1500]{2,1,0:T(4,128)(2,1)} %collective-permute-done.3), channel_id=1, source_target_pairs={{0,4},{4,8},{8,12},{12,16},{16,20},{20,24},{24,28},{28,0},{1,5},{5... | collective-permute-start | bytes 2880008 | tf_op jit(solution)/shard_map/ppermute | solution.py:16
  153.6 1.0 copy-start.4
  154.5 22.3 %collective-permute-start.5 = (bf16[80,4,1500]{2,1,0:T(4,128)(2,1)S(1)}, bf16[80,4,1500]{2,1,0:T(4,128)(2,1)}, u32[]{:S(2)}, u32[]{:S(2)}) collective-permute-start(bf16[80,4,1500]{2,1,0:T(4,128)(2,1)S(1)} %collective-permute-done.4), channel_id=1, source_target_pairs={{0,4},{4,8},{8,12},{12,16},{16,20},{20,24},{24,28},{28,0},{1,5},{5... | collective-permute-start | bytes 2880008 | tf_op jit(solution)/shard_map/ppermute | solution.py:16
  176.8 21.6 %collective-permute-start.6 = (bf16[80,4,1500]{2,1,0:T(4,128)(2,1)}, bf16[80,4,1500]{2,1,0:T(4,128)(2,1)}, u32[]{:S(2)}, u32[]{:S(2)}) collective-permute-start(bf16[80,4,1500]{2,1,0:T(4,128)(2,1)} %collective-permute-done.5), channel_id=1, source_target_pairs={{0,4},{4,8},{8,12},{12,16},{16,20},{20,24},{24,28},{28,0},{1,5},{5... | collective-permute-start | bytes 2880008 | tf_op jit(solution)/shard_map/ppermute | solution.py:16
  179.4 42.9 %copy-start.5 = (bf16[80,4,1500]{2,1,0:T(4,128)(2,1)S(1)}, bf16[80,4,1500]{2,1,0:T(4,128)(2,1)}, u32[]{:S(2)}) copy-start(bf16[80,4,1500]{2,1,0:T(4,128)(2,1)} %copy-done.4) | copy-start | bytes 2880004
  179.4 49.2 %copy-start.3 = (bf16[80,4,1500]{2,1,0:T(4,128)(2,1)S(1)}, bf16[80,4,1500]{2,1,0:T(4,128)(2,1)}, u32[]{:S(2)}) copy-start(bf16[80,4,1500]{2,1,0:T(4,128)(2,1)} %copy-done.2) | copy-start | bytes 2880004
  265.9 21.9 %copy-start.6 = (f32[2]{0:T(128)S(1)}, f32[2]{0:T(128)}, u32[]{:S(2)}) copy-start(f32[2]{0:T(128)} %param.11) | copy-start | bytes 28
Sparse Core Ops, SparseCore 0:
  11.7 60.1 all-gather.2
  109.1 48.9 all-gather.4
